TPU v7x, 32 devices: a whole 2x2x4 slice. The times are simulated.
32 devices in a mesh: pair: 8 (over y, x, core), row: 4 (over z).
Axes of the slice: x: 2, y: 2, z: 4, core: 2. Of those that a mesh axis runs over, the one named last changes fastest.
Arguments:
- amplitudes: bfloat16 [3, 160, 32, 5120], P(None, 'pair', 'row'), may hold values from -6 to 6
- integrals: bfloat16 [3, 5120, 5120], P(None, 'row', 'pair'), may hold values from -0.078125 to 0.078125
- occupied_irrep: int32 [32], replicated, may hold values from 0 to 7
- virtual_order: int32 [1280], replicated, may hold values from 0 to 1279, each once
- block_irreps: int32 [3], replicated, may hold values from 0 to 7
- occupied_energy: float32 [32], replicated, may hold values from -2 to -0.5
- virtual_energy: float32 [1280], replicated, may hold values from 1 to 4
Outputs:
- update: float32 [3, 160, 32, 5120], P(None, None, 'row', 'pair')
Inputs may be any that keep to these rules, and one draw needn't show every extreme that they name: virtual_order holds every virtual orbital once; entries g * 160 to g * 160 + 159 are the virtual orbitals of irrep g.
All inputs are finite; a program needn't handle non-finite values.
Results may differ from a plain program's by a relative error of at most 0.0003.
Values may be sent and summed in bfloat16 or wider, within the bound.
A program may use at most 128 MiB of HBM per device.

v0:
```python
import jax
import jax.numpy as jnp
from jax import lax
from jax.sharding import PartitionSpec as P

VIRG = 160


def shift_table(occupied_irrep, virtual_order, block_irreps, occupied_energy, virtual_energy):
    count_virt = virtual_energy.shape[0]
    orbital_ids = jnp.arange(count_virt, dtype=jnp.int32)
    matches = virtual_order[:, None] == orbital_ids[None, :]
    slot_energy = jnp.sum(jnp.where(matches, virtual_energy[None, :], jnp.float32(0.0)), axis=1)
    irrep_count = count_virt // VIRG
    energy_grid = slot_energy.reshape(irrep_count, VIRG)
    pair_irrep = jnp.bitwise_xor(block_irreps[:, None], occupied_irrep[None, :])
    irrep_ids = jnp.arange(irrep_count, dtype=jnp.int32)
    chosen = pair_irrep[:, None, None, :] == irrep_ids[None, :, None, None]
    picked = jnp.sum(jnp.where(chosen, energy_grid[None, :, :, None], jnp.float32(0.0)), axis=1)
    return picked - occupied_energy[None, None, :]


def body(
    amplitudes,
    integrals,
    occupied_irrep,
    virtual_order,
    block_irreps,
    occupied_energy,
    virtual_energy,
):
    block_count, virt_local, occ_local, pair_width = amplitudes.shape
    column_width = integrals.shape[2]
    shift = shift_table(
        occupied_irrep, virtual_order, block_irreps, occupied_energy, virtual_energy
    )
    occ_start = lax.axis_index("row") * occ_local
    col_start = lax.axis_index("pair") * column_width
    results = []
    for block in range(block_count):
        whole_rows = lax.all_gather(integrals[block], "row", axis=0, tiled=True)
        piece = lax.all_gather(amplitudes[block], "pair", axis=0, tiled=True)
        flat = piece.reshape(piece.shape[0] * piece.shape[1], piece.shape[2])
        product = jnp.dot(flat, whole_rows, preferred_element_type=jnp.float32)
        cycle_term = product.reshape(piece.shape[0], piece.shape[1], whole_rows.shape[1])
        row_shift = lax.dynamic_slice_in_dim(shift[block], occ_start, occ_local, 1)
        col_shift = lax.dynamic_slice_in_dim(
            shift[block].reshape(pair_width), col_start, column_width, 0
        )
        denominator = row_shift[:, :, None] + col_shift[None, None, :]
        results.append(cycle_term / denominator)
    return jnp.stack(results)


def solution(mesh):
    placed = (P(None, "pair", "row", None), P(None, "row", "pair"), P(), P(), P(), P(), P())
    return jax.shard_map(
        body, mesh=mesh, in_specs=placed, out_specs=P(None, None, "row", "pair"), check_vma=False
    )
```

profile of v0, /device:TPU:0, one launch (start us, length us, event | category | flops | bytes accessed | tf_op | source)
XLA Modules:
  0.0 626.3 jit_solution(1180767231952461776)
XLA Ops:
  6.5 4.8 fusion.21
  11.5 4.7 slice_bitcast_fusion.2
  16.3 0.7 all-gather.15.cloned.1.call-update
  17.0 0.5 all-gather.13.cloned.1.call-update
  17.6 0.5 all-gather.23.cloned.1.call-update
  18.2 0.5 all-gather.21.cloned.1.call-update
  18.7 1.0 select_reduce_fusion
  19.7 0.1 broadcast_in_dim.51
  19.9 0.2 select_reduce_fusion.1
  20.0 0.1 broadcast_subtract_fusion
  20.1 0.1 copy.22
  20.2 0.1 reshape_squeeze.10
  20.3 0.1 copy.21
  20.4 0.1 copy.19
  20.6 0.1 reshape_squeeze.9
  20.6 0.1 dynamic_slice.21
  20.7 0.1 dynamic_slice.19
  20.8 0.1 copy.18
  20.9 0.1 copy.25
  21.0 0.1 reshape_squeeze.11
  21.1 0.1 dynamic_slice.23
  21.2 0.1 copy.24
  21.3 112.6 %all-gather.19.cloned.1.call-done = bf16[1,5120,640]{2,1,0:T(8,128)(2,1)} async-done(((bf16[1,1280,640]{2,1,0:T(8,128)(2,1)}), bf16[1,5120,640]{2,1,0:T(8,128)(2,1)}) %all-gather.19.cloned.1.call-update) | async-done | bytes 6553616 | tf_op jit(solution)/shard_map/all_gather | solution.py:41
  133.9 74.5 %all-gather.17.cloned.1.call-done = bf16[1,160,8,5120]{3,2,0,1:T(8,128)(2,1)} async-done(((bf16[1,20,8,5120]{3,2,0,1:T(8,128)(2,1)}), bf16[1,160,8,5120]{3,2,0,1:T(8,128)(2,1)}) %all-gather.17.cloned.1.call-update) | async-done | bytes 13107216 | tf_op jit(solution)/shard_map/all_gather | solution.py:42
  208.4 15.1 %divide_bitcast_fusion.1 = f32[1,160,8,640]{3,2,1,0:T(8,128)S(1)} fusion(bf16[1,5120,640]{2,1,0:T(8,128)(2,1)} %all-gather.19.cloned.1.call-done, bf16[1,160,8,5120]{3,2,0,1:T(8,128)(2,1)} %all-gather.17.cloned.1.call-done, f32[640]{0:T(1024)S(1)} %dynamic_slice.21, f32[160,8]{1,0:T(8,128)S(1)} %copy.21), kind=kOutput, calls=%fused_computation.13 | convolution fusion | flops 8390246400 | bytes 22945280 | tf_op jit(solution)/shard_map/dot_general | solution.py:44
  223.6 106.1 %all-gather.15.cloned.1.call-done = bf16[1,5120,640]{2,1,0:T(8,128)(2,1)} async-done(((bf16[1,1280,640]{2,1,0:T(8,128)(2,1)}), bf16[1,5120,640]{2,1,0:T(8,128)(2,1)}) %all-gather.15.cloned.1.call-update) | async-done | bytes 6553616 | tf_op jit(solution)/shard_map/all_gather | solution.py:41
  329.7 74.4 %all-gather.13.cloned.1.call-done = bf16[1,160,8,5120]{3,2,0,1:T(8,128)(2,1)} async-done(((bf16[1,20,8,5120]{3,2,0,1:T(8,128)(2,1)}), bf16[1,160,8,5120]{3,2,0,1:T(8,128)(2,1)}) %all-gather.13.cloned.1.call-update) | async-done | bytes 13107216 | tf_op jit(solution)/shard_map/all_gather | solution.py:42
  404.0 16.0 %divide_bitcast_fusion.2 = f32[1,160,8,640]{3,2,1,0:T(8,128)} fusion(bf16[1,5120,640]{2,1,0:T(8,128)(2,1)} %all-gather.15.cloned.1.call-done, bf16[1,160,8,5120]{3,2,0,1:T(8,128)(2,1)} %all-gather.13.cloned.1.call-done, f32[640]{0:T(1024)S(1)} %dynamic_slice.19, f32[160,8]{1,0:T(8,128)S(1)} %copy.18), kind=kOutput, calls=%fused_computation.14 | convolution fusion | flops 8390246400 | bytes 22945280 | tf_op jit(solution)/shard_map/dot_general | solution.py:44
  420.0 105.1 %all-gather.23.cloned.1.call-done = bf16[1,5120,640]{2,1,0:T(8,128)(2,1)} async-done(((bf16[1,1280,640]{2,1,0:T(8,128)(2,1)}), bf16[1,5120,640]{2,1,0:T(8,128)(2,1)}) %all-gather.23.cloned.1.call-update) | async-done | bytes 6553616 | tf_op jit(solution)/shard_map/all_gather | solution.py:41
  525.1 74.4 %all-gather.21.cloned.1.call-done = bf16[1,160,8,5120]{3,2,0,1:T(8,128)(2,1)} async-done(((bf16[1,20,8,5120]{3,2,0,1:T(8,128)(2,1)}), bf16[1,160,8,5120]{3,2,0,1:T(8,128)(2,1)}) %all-gather.21.cloned.1.call-update) | async-done | bytes 13107216 | tf_op jit(solution)/shard_map/all_gather | solution.py:42
  599.5 15.3 %divide_bitcast_fusion = f32[1,160,8,640]{3,2,1,0:T(8,128)S(1)} fusion(bf16[1,5120,640]{2,1,0:T(8,128)(2,1)} %all-gather.23.cloned.1.call-done, bf16[1,160,8,5120]{3,2,0,1:T(8,128)(2,1)} %all-gather.21.cloned.1.call-done, f32[640]{0:T(1024)S(1)} %dynamic_slice.23, f32[160,8]{1,0:T(8,128)S(1)} %copy.24), kind=kOutput, calls=%fused_computation.12 | convolution fusion | flops 8390246400 | bytes 22945280 | tf_op jit(solution)/shard_map/dot_general | solution.py:44
  614.8 4.7 pad_maximum_fusion
  (26 shorter events, 0.4 us)
Async XLA Ops:
  6.5 127.4 %all-gather.19.cloned.1.call-start = ((), (), s32[]{:S(2)}) async-start(), calls=%async_computation.3 | async-start | bytes 8192000 | tf_op jit(solution)/shard_map/all_gather | solution.py:41
  11.4 197.0 %all-gather.17.cloned.1.call-start = ((), (), s32[]{:S(2)}) async-start(), calls=%async_computation.2 | async-start | bytes 14745600 | tf_op jit(solution)/shard_map/all_gather | solution.py:42
  16.2 2.5 copy-start.1
  16.2 2.5 copy-start.2
  16.2 3.6 copy-start.4
  16.2 3.6 copy-start.5
  16.2 3.9 copy-start.3
  16.2 313.4 %all-gather.15.cloned.1.call-start = ((), (), s32[]{:S(2)}) async-start(), calls=%async_computation.1 | async-start | bytes 8192000 | tf_op jit(solution)/shard_map/all_gather | solution.py:41
  17.0 387.1 %all-gather.13.cloned.1.call-start = ((), (), s32[]{:S(2)}) async-start(), calls=%async_computation | async-start | bytes 14745600 | tf_op jit(solution)/shard_map/all_gather | solution.py:42
  17.5 507.6 %all-gather.23.cloned.1.call-start = ((), (), s32[]{:S(2)}) async-start(), calls=%async_computation.5 | async-start | bytes 8192000 | tf_op jit(solution)/shard_map/all_gather | solution.py:41
  18.1 581.3 %all-gather.21.cloned.1.call-start = ((), (), s32[]{:S(2)}) async-start(), calls=%async_computation.4 | async-start | bytes 14745600 | tf_op jit(solution)/shard_map/all_gather | solution.py:42
  599.5 15.3 %copy-start = (f32[1,160,8,640]{3,2,1,0:T(8,128)S(1)}, f32[1,160,8,640]{3,2,1,0:T(8,128)}, u32[]{:S(2)}) copy-start(f32[1,160,8,640]{3,2,1,0:T(8,128)} %divide_bitcast_fusion.2) | copy-start | bytes 9830404
Sparse Core Ops, SparseCore 0:
  11.5 122.3 all-gather.18
  135.8 72.5 all-gather.16
  210.0 119.6 all-gather.14
  331.4 72.5 all-gather.12
  405.4 119.6 all-gather.22
  526.9 72.5 all-gather.20
where the time goes:
time: 626 us
  waiting for transfers between devices  549 us (88%)
  matrix products  46.4 us (7%)
  between operations  13.6 us (2%)
  local copies, waits for them, and re-layouts  10.8 us (2%)
    all_gather x3, waiting for transfers between devices, body(): whole_rows = lax.all_gather(integrals[block], 'row', axis=0, tiled=True)  324 us
    all_gather x3, waiting for transfers between devices, body(): piece = lax.all_gather(amplitudes[block], 'pair', axis=0, tiled=True)  223 us
    dot_general x3, matrix products, body(): product = jnp.dot(flat, whole_rows, preferred_element_type=jnp.float32)  46.4 us
  transfers between devices with their start and end apart: 6, of which 6 were waited for; matrix products, arithmetic and copies ran while one was open for 6% of the time, Pallas kernels for 0%

commit v1 on v0

--- a/solution.py
+++ b/solution.py
@@ -39,7 +39,14 @@
     results = []
     for block in range(block_count):
         whole_rows = lax.all_gather(integrals[block], "row", axis=0, tiled=True)
-        piece = lax.all_gather(amplitudes[block], "pair", axis=0, tiled=True)
+        ring = [amplitudes[block]]
+        for hop in range(7):
+            ring.append(lax.ppermute(ring[-1], "pair", [(dev, (dev + 1) % 8) for dev in range(8)]))
+        piece = jnp.roll(
+            jnp.concatenate(ring[::-1], axis=0),
+            (lax.axis_index("pair") + 1) * ring[0].shape[0],
+            axis=0,
+        )
         flat = piece.reshape(piece.shape[0] * piece.shape[1], piece.shape[2])
         product = jnp.dot(flat, whole_rows, preferred_element_type=jnp.float32)
         cycle_term = product.reshape(piece.shape[0], piece.shape[1], whole_rows.shape[1])

time: 626 us -> 474 us (0.76)
  waiting for transfers between devices: 549 us -> 339 us
  local copies, waits for them, and re-layouts: 10.8 us -> 53.8 us
  matrix products: 46.4 us -> 55.8 us
    ppermute x0 -> x21, waiting for transfers between devices: none -> 338 us  [body(): lax.ppermute(ring[-1], 'pair', [(dev, (dev + 1) % 8) for dev in range(8)])]
    all_gather x3, waiting for transfers between devices: 324 us -> 0.02 us  [body(): whole_rows = lax.all_gather(integrals[block], 'row', axis=0, tiled=True)]
    all_gather x3 -> x0, waiting for transfers between devices: 223 us -> none  [body(): piece = lax.all_gather(amplitudes[block], 'pair', axis=0, tiled=True)]
    unnamed x13 -> x71, local copies, waits for them, and re-layouts: 4.74 us -> 41.5 us
    dot_general x3, matrix products: 46.4 us -> 55.8 us  [body(): product = jnp.dot(flat, whole_rows, preferred_element_type=jnp.float32)]
  transfers between devices with their start and end apart: 6 -> 24, of which waited for: 6 -> 21; matrix products, arithmetic and copies ran while one was open for 6% -> 18% of each run, Pallas kernels for 0% -> 0%
where the time goes in v1:
time: 474 us
  waiting for transfers between devices  339 us (72%)
  matrix products  55.8 us (12%)
  local copies, waits for them, and re-layouts  53.8 us (11%)
  between operations  13.3 us (3%)
  other arithmetic  8.71 us (2%)
    ppermute x21, waiting for transfers between devices, body(): lax.ppermute(ring[-1], 'pair', [(dev, (dev + 1) % 8) for dev in range(8)])  338 us
    dot_general x3, matrix products, body(): product = jnp.dot(flat, whole_rows, preferred_element_type=jnp.float32)  55.8 us
    unnamed x71, local copies, waits for them, and re-layouts  41.5 us
  transfers between devices with their start and end apart: 24, of which 21 were waited for; matrix products, arithmetic and copies ran while one was open for 18% of the time, Pallas kernels for 0%

profile of v1, /device:TPU:0, one launch (start us, length us, event | category | flops | bytes accessed | tf_op | source)
XLA Modules:
  0.0 473.9 jit_solution(12392230026735193600)
XLA Ops:
  6.5 4.8 %fusion.30 = (bf16[1,1280,640]{2,1,0:T(8,128)(2,1)}, bf16[1,1280,640]{2,1,0:T(8,128)(2,1)}, bf16[1,1280,640]{2,1,0:T(8,128)(2,1)}) fusion(bf16[3,1280,640]{2,1,0:T(8,128)(2,1)} %param.10), kind=kLoop, calls=%fused_computation.61 | loop fusion | bytes 9830400 | tf_op jit(solution)/shard_map/slice | solution.py:41
  12.2 2.7 slice_bitcast_fusion.2
  18.1 19.0 %collective-permute-done.14 = bf16[20,8,5120]{2,1,0:T(8,128)(2,1)S(1)} collective-permute-done((bf16[20,8,5120]{2,1,0:T(8,128)(2,1)S(1)}, bf16[20,8,5120]{2,1,0:T(8,128)(2,1)S(1)}, u32[]{:S(2)}, u32[]{:S(2)}) %collective-permute-start.14) | collective-permute-done | bytes 1638432 | tf_op jit(solution)/shard_map/ppermute | solution.py:44
  37.1 17.5 %collective-permute-done.7 = bf16[20,8,5120]{2,1,0:T(8,128)(2,1)S(1)} collective-permute-done((bf16[20,8,5120]{2,1,0:T(8,128)(2,1)S(1)}, bf16[20,8,5120]{2,1,0:T(8,128)(2,1)S(1)}, u32[]{:S(2)}, u32[]{:S(2)}) %collective-permute-start.7) | collective-permute-done | bytes 1638432 | tf_op jit(solution)/shard_map/ppermute | solution.py:44
  54.7 17.6 %collective-permute-done = bf16[20,8,5120]{2,1,0:T(8,128)(2,1)S(1)} collective-permute-done((bf16[20,8,5120]{2,1,0:T(8,128)(2,1)S(1)}, bf16[20,8,5120]{2,1,0:T(8,128)(2,1)S(1)}, u32[]{:S(2)}, u32[]{:S(2)}) %collective-permute-start) | collective-permute-done | bytes 1638432 | tf_op jit(solution)/shard_map/ppermute | solution.py:44
  72.2 17.6 %collective-permute-done.15 = bf16[20,8,5120]{2,1,0:T(8,128)(2,1)S(1)} collective-permute-done((bf16[20,8,5120]{2,1,0:T(8,128)(2,1)S(1)}, bf16[20,8,5120]{2,1,0:T(8,128)(2,1)S(1)}, u32[]{:S(2)}, u32[]{:S(2)}) %collective-permute-start.15) | collective-permute-done | bytes 1638432 | tf_op jit(solution)/shard_map/ppermute | solution.py:44
  89.8 17.5 %collective-permute-done.8 = bf16[20,8,5120]{2,1,0:T(8,128)(2,1)S(1)} collective-permute-done((bf16[20,8,5120]{2,1,0:T(8,128)(2,1)S(1)}, bf16[20,8,5120]{2,1,0:T(8,128)(2,1)S(1)}, u32[]{:S(2)}, u32[]{:S(2)}) %collective-permute-start.8) | collective-permute-done | bytes 1638432 | tf_op jit(solution)/shard_map/ppermute | solution.py:44
  107.4 17.5 %collective-permute-done.1 = bf16[20,8,5120]{2,1,0:T(8,128)(2,1)S(1)} collective-permute-done((bf16[20,8,5120]{2,1,0:T(8,128)(2,1)S(1)}, bf16[20,8,5120]{2,1,0:T(8,128)(2,1)S(1)}, u32[]{:S(2)}, u32[]{:S(2)}) %collective-permute-start.1) | collective-permute-done | bytes 1638432 | tf_op jit(solution)/shard_map/ppermute | solution.py:44
  126.1 16.4 %collective-permute-done.16 = bf16[20,8,5120]{2,1,0:T(8,128)(2,1)S(1)} collective-permute-done((bf16[20,8,5120]{2,1,0:T(8,128)(2,1)S(1)}, bf16[20,8,5120]{2,1,0:T(8,128)(2,1)S(1)}, u32[]{:S(2)}, u32[]{:S(2)}) %collective-permute-start.16) | collective-permute-done | bytes 1638432 | tf_op jit(solution)/shard_map/ppermute | solution.py:44
  142.5 17.5 %collective-permute-done.9 = bf16[20,8,5120]{2,1,0:T(8,128)(2,1)S(1)} collective-permute-done((bf16[20,8,5120]{2,1,0:T(8,128)(2,1)S(1)}, bf16[20,8,5120]{2,1,0:T(8,128)(2,1)S(1)}, u32[]{:S(2)}, u32[]{:S(2)}) %collective-permute-start.9) | collective-permute-done | bytes 1638432 | tf_op jit(solution)/shard_map/ppermute | solution.py:44
  160.0 17.5 %collective-permute-done.2 = bf16[20,8,5120]{2,1,0:T(8,128)(2,1)S(1)} collective-permute-done((bf16[20,8,5120]{2,1,0:T(8,128)(2,1)S(1)}, bf16[20,8,5120]{2,1,0:T(8,128)(2,1)S(1)}, u32[]{:S(2)}, u32[]{:S(2)}) %collective-permute-start.2) | collective-permute-done | bytes 1638432 | tf_op jit(solution)/shard_map/ppermute | solution.py:44
  177.6 17.5 %collective-permute-done.17 = bf16[20,8,5120]{2,1,0:T(8,128)(2,1)S(1)} collective-permute-done((bf16[20,8,5120]{2,1,0:T(8,128)(2,1)S(1)}, bf16[20,8,5120]{2,1,0:T(8,128)(2,1)S(1)}, u32[]{:S(2)}, u32[]{:S(2)}) %collective-permute-start.17) | collective-permute-done | bytes 1638432 | tf_op jit(solution)/shard_map/ppermute | solution.py:44
  195.1 17.6 %collective-permute-done.10 = bf16[20,8,5120]{2,1,0:T(8,128)(2,1)} collective-permute-done((bf16[20,8,5120]{2,1,0:T(8,128)(2,1)S(1)}, bf16[20,8,5120]{2,1,0:T(8,128)(2,1)}, u32[]{:S(2)}, u32[]{:S(2)}) %collective-permute-start.10) | collective-permute-done | bytes 1638432 | tf_op jit(solution)/shard_map/ppermute | solution.py:44
  212.8 17.6 %collective-permute-done.3 = bf16[20,8,5120]{2,1,0:T(8,128)(2,1)} collective-permute-done((bf16[20,8,5120]{2,1,0:T(8,128)(2,1)S(1)}, bf16[20,8,5120]{2,1,0:T(8,128)(2,1)}, u32[]{:S(2)}, u32[]{:S(2)}) %collective-permute-start.3) | collective-permute-done | bytes 1638432 | tf_op jit(solution)/shard_map/ppermute | solution.py:44
  230.4 17.5 %collective-permute-done.18 = bf16[20,8,5120]{2,1,0:T(8,128)(2,1)} collective-permute-done((bf16[20,8,5120]{2,1,0:T(8,128)(2,1)S(1)}, bf16[20,8,5120]{2,1,0:T(8,128)(2,1)}, u32[]{:S(2)}, u32[]{:S(2)}) %collective-permute-start.18) | collective-permute-done | bytes 1638432 | tf_op jit(solution)/shard_map/ppermute | solution.py:44
  248.0 17.5 %collective-permute-done.11 = bf16[20,8,5120]{2,1,0:T(8,128)(2,1)} collective-permute-done((bf16[20,8,5120]{2,1,0:T(8,128)(2,1)}, bf16[20,8,5120]{2,1,0:T(8,128)(2,1)}, u32[]{:S(2)}, u32[]{:S(2)}) %collective-permute-start.11) | collective-permute-done | bytes 1638432 | tf_op jit(solution)/shard_map/ppermute | solution.py:44
  265.5 17.6 %collective-permute-done.4 = bf16[20,8,5120]{2,1,0:T(8,128)(2,1)} collective-permute-done((bf16[20,8,5120]{2,1,0:T(8,128)(2,1)}, bf16[20,8,5120]{2,1,0:T(8,128)(2,1)}, u32[]{:S(2)}, u32[]{:S(2)}) %collective-permute-start.4) | collective-permute-done | bytes 1638432 | tf_op jit(solution)/shard_map/ppermute | solution.py:44
  283.0 17.6 %collective-permute-done.19 = bf16[20,8,5120]{2,1,0:T(8,128)(2,1)} collective-permute-done((bf16[20,8,5120]{2,1,0:T(8,128)(2,1)}, bf16[20,8,5120]{2,1,0:T(8,128)(2,1)}, u32[]{:S(2)}, u32[]{:S(2)}) %collective-permute-start.19) | collective-permute-done | bytes 1638432 | tf_op jit(solution)/shard_map/ppermute | solution.py:44
  304.4 13.7 %collective-permute-done.12 = bf16[20,8,5120]{2,1,0:T(8,128)(2,1)} collective-permute-done((bf16[20,8,5120]{2,1,0:T(8,128)(2,1)}, bf16[20,8,5120]{2,1,0:T(8,128)(2,1)}, u32[]{:S(2)}, u32[]{:S(2)}) %collective-permute-start.12) | collective-permute-done | bytes 1638432 | tf_op jit(solution)/shard_map/ppermute | solution.py:44
  318.1 17.6 %collective-permute-done.5 = bf16[20,8,5120]{2,1,0:T(8,128)(2,1)} collective-permute-done((bf16[20,8,5120]{2,1,0:T(8,128)(2,1)}, bf16[20,8,5120]{2,1,0:T(8,128)(2,1)}, u32[]{:S(2)}, u32[]{:S(2)}) %collective-permute-start.5) | collective-permute-done | bytes 1638432 | tf_op jit(solution)/shard_map/ppermute | solution.py:44
  335.7 17.6 %collective-permute-done.20 = bf16[20,8,5120]{2,1,0:T(8,128)(2,1)} collective-permute-done((bf16[20,8,5120]{2,1,0:T(8,128)(2,1)}, bf16[20,8,5120]{2,1,0:T(8,128)(2,1)}, u32[]{:S(2)}, u32[]{:S(2)}) %collective-permute-start.20) | collective-permute-done | bytes 1638432 | tf_op jit(solution)/shard_map/ppermute | solution.py:44
  353.2 2.7 constant_dynamic-update-slice_fusion.23
  358.6 2.7 constant_dynamic-update-slice_fusion.21
  366.7 4.0 collective-permute-done.13
  372.0 2.8 constant_dynamic-update-slice_fusion.14
  384.0 4.2 collective-permute-done.6
  389.5 2.9 constant_dynamic-update-slice_fusion.6
  392.4 2.7 constant_dynamic-update-slice_fusion.5
  404.0 17.3 %divide_bitcast_fusion.2 = f32[1,160,8,640]{3,2,1,0:T(8,128)S(1)} fusion(f32[640]{0:T(1024)S(1)} %dynamic_slice.22, f32[160,8]{1,0:T(8,128)S(1)} %copy.11, bf16[1,5120,640]{2,1,0:T(8,128)(2,1)} %all-gather.7.cloned.1.call-done, s32[]{:T(128)S(6)} %select_n.37, bf16[160,8,5120]{2,1,0:T(8,128)(2,1)} %get-tuple-element.6), kind=kOutput, calls=%fused_computation.20 | convolution fusion | flops 8396800000 | bytes 22945284 | tf_op jit(solution)/shard_map/dot_general | solution.py:51
  421.4 19.1 %divide_bitcast_fusion.1 = f32[1,160,8,640]{3,2,1,0:T(8,128)} fusion(f32[640]{0:T(1024)S(1)} %dynamic_slice.24, f32[160,8]{1,0:T(8,128)S(1)} %copy-done.16, bf16[1,5120,640]{2,1,0:T(8,128)(2,1)} %all-gather.9.cloned.1.call-done, s32[]{:T(128)S(6)} %select_n.37, bf16[160,8,5120]{2,1,0:T(8,128)(2,1)} %get-tuple-element.8), kind=kOutput, calls=%fused_computation.19 | convolution fusion | flops 8396800000 | bytes 22945284 | tf_op jit(solution)/shard_map/dot_general | solution.py:51
  440.6 19.3 %divide_bitcast_fusion = f32[1,160,8,640]{3,2,1,0:T(8,128)} fusion(f32[640]{0:T(1024)S(1)} %dynamic_slice.26, f32[160,8]{1,0:T(8,128)S(1)} %copy-done.17, bf16[1,5120,640]{2,1,0:T(8,128)(2,1)} %all-gather.11.cloned.1.call-done, s32[]{:T(128)S(6)} %select_n.37, bf16[160,8,5120]{2,1,0:T(8,128)(2,1)} %get-tuple-element.7), kind=kOutput, calls=%fused_computation.18 | convolution fusion | flops 8396800000 | bytes 22945284 | tf_op jit(solution)/shard_map/dot_general | solution.py:51
  459.9 7.4 %pad_maximum_fusion = f32[3,160,8,640]{3,2,1,0:T(8,128)} fusion(f32[1,160,8,640]{3,2,1,0:T(8,128)} %divide_bitcast_fusion, f32[1,160,8,640]{3,2,1,0:T(8,128)} %divide_bitcast_fusion.1, f32[1,160,8,640]{3,2,1,0:T(8,128)S(1)} %divide_bitcast_fusion.2), kind=kLoop, calls=%fused_computation.12 | loop fusion | flops 4915200 | bytes 19660800 | tf_op jit(solution)/shard_map/stack | solution.py:59
  (120 shorter events, 37.8 us)
Async XLA Ops:
  6.5 397.5 %all-gather.7.cloned.1.call-start = ((), (), s32[]{:S(2)}) async-start(), calls=%async_computation | async-start | bytes 8192000 | tf_op jit(solution)/shard_map/all_gather | solution.py:41
  11.3 289.2 %copy-start.18 = (f32[1280]{0:T(1024)S(1)}, f32[1280]{0:T(1024)}, u32[]{:S(2)}) copy-start(f32[1280]{0:T(1024)} %param.15) | copy-start | bytes 15364
  11.3 289.2 %copy-start.19 = (s32[1280]{0:T(1024)S(1)}, s32[1280]{0:T(1024)}, u32[]{:S(2)}) copy-start(s32[1280]{0:T(1024)} %param.12) | copy-start | bytes 15364
  11.3 290.3 %copy-start.21 = (s32[32]{0:T(128)S(1)}, s32[32]{0:T(128)}, u32[]{:S(2)}) copy-start(s32[32]{0:T(128)} %param.11) | copy-start | bytes 388
  11.4 290.3 %copy-start.22 = (s32[3]{0:T(128)S(1)}, s32[3]{0:T(128)}, u32[]{:S(2)}) copy-start(s32[3]{0:T(128)} %param.13) | copy-start | bytes 40
  11.4 290.5 %copy-start.20 = (f32[32]{0:T(128)S(1)}, f32[32]{0:T(128)}, u32[]{:S(2)}) copy-start(f32[32]{0:T(128)} %param.14) | copy-start | bytes 388
  11.4 410.0 %all-gather.9.cloned.1.call-start = ((), (), s32[]{:S(2)}) async-start(), calls=%async_computation.1 | async-start | bytes 8192000 | tf_op jit(solution)/shard_map/all_gather | solution.py:41
  12.1 428.4 %all-gather.11.cloned.1.call-start = ((), (), s32[]{:S(2)}) async-start(), calls=%async_computation.2 | async-start | bytes 8192000 | tf_op jit(solution)/shard_map/all_gather | solution.py:41
  14.9 22.2 %collective-permute-start.14 = (bf16[20,8,5120]{2,1,0:T(8,128)(2,1)S(1)}, bf16[20,8,5120]{2,1,0:T(8,128)(2,1)S(1)}, u32[]{:S(2)}, u32[]{:S(2)}) collective-permute-start(bf16[20,8,5120]{2,1,0:T(8,128)(2,1)S(1)} %get-tuple-element.10), channel_id=1, source_target_pairs={{0,4},{4,8},{8,12},{12,16},{16,20},{20,24},{24,28},{28,0},{1,5},{5... | collective-permute-start | bytes 4915208 | tf_op jit(solution)/shard_map/ppermute | solution.py:44
  15.4 39.2 %collective-permute-start.7 = (bf16[20,8,5120]{2,1,0:T(8,128)(2,1)S(1)}, bf16[20,8,5120]{2,1,0:T(8,128)(2,1)S(1)}, u32[]{:S(2)}, u32[]{:S(2)}) collective-permute-start(bf16[20,8,5120]{2,1,0:T(8,128)(2,1)S(1)} %get-tuple-element.11), channel_id=1, source_target_pairs={{0,4},{4,8},{8,12},{12,16},{16,20},{20,24},{24,28},{28,0},{1,5},{5... | collective-permute-start | bytes 4915208 | tf_op jit(solution)/shard_map/ppermute | solution.py:44
  18.0 54.2 %collective-permute-start = (bf16[20,8,5120]{2,1,0:T(8,128)(2,1)S(1)}, bf16[20,8,5120]{2,1,0:T(8,128)(2,1)S(1)}, u32[]{:S(2)}, u32[]{:S(2)}) collective-permute-start(bf16[20,8,5120]{2,1,0:T(8,128)(2,1)S(1)} %get-tuple-element.9), channel_id=1, source_target_pairs={{0,4},{4,8},{8,12},{12,16},{16,20},{20,24},{24,28},{28,0},{1,5},{5... | collective-permute-start | bytes 4915208 | tf_op jit(solution)/shard_map/ppermute | solution.py:44
  37.1 140.4 %copy-start.2 = (bf16[20,8,5120]{2,1,0:T(8,128)(2,1)}, bf16[20,8,5120]{2,1,0:T(8,128)(2,1)S(1)}, u32[]{:S(2)}) copy-start(bf16[20,8,5120]{2,1,0:T(8,128)(2,1)S(1)} %collective-permute-done.14) | copy-start | bytes 4915204
  37.1 52.7 %collective-permute-start.15 = (bf16[20,8,5120]{2,1,0:T(8,128)(2,1)S(1)}, bf16[20,8,5120]{2,1,0:T(8,128)(2,1)S(1)}, u32[]{:S(2)}, u32[]{:S(2)}) collective-permute-start(bf16[20,8,5120]{2,1,0:T(8,128)(2,1)S(1)} %collective-permute-done.14), channel_id=1, source_target_pairs={{0,4},{4,8},{8,12},{12,16},{16,20},{20,24},{24,28},{28,0},{1,5},{5... | collective-permute-start | bytes 4915208 | tf_op jit(solution)/shard_map/ppermute | solution.py:44
  54.7 52.7 %collective-permute-start.8 = (bf16[20,8,5120]{2,1,0:T(8,128)(2,1)S(1)}, bf16[20,8,5120]{2,1,0:T(8,128)(2,1)S(1)}, u32[]{:S(2)}, u32[]{:S(2)}) collective-permute-start(bf16[20,8,5120]{2,1,0:T(8,128)(2,1)S(1)} %collective-permute-done.7), channel_id=1, source_target_pairs={{0,4},{4,8},{8,12},{12,16},{16,20},{20,24},{24,28},{28,0},{1,5},{5... | collective-permute-start | bytes 4915208 | tf_op jit(solution)/shard_map/ppermute | solution.py:44
  72.2 52.7 %collective-permute-start.1 = (bf16[20,8,5120]{2,1,0:T(8,128)(2,1)S(1)}, bf16[20,8,5120]{2,1,0:T(8,128)(2,1)S(1)}, u32[]{:S(2)}, u32[]{:S(2)}) collective-permute-start(bf16[20,8,5120]{2,1,0:T(8,128)(2,1)S(1)} %collective-permute-done), channel_id=1, source_target_pairs={{0,4},{4,8},{8,12},{12,16},{16,20},{20,24},{24,28},{28,0},{1,5},{5... | collective-permute-start | bytes 4915208 | tf_op jit(solution)/shard_map/ppermute | solution.py:44
  89.8 140.5 %copy-start.8 = (bf16[20,8,5120]{2,1,0:T(8,128)(2,1)}, bf16[20,8,5120]{2,1,0:T(8,128)(2,1)S(1)}, u32[]{:S(2)}) copy-start(bf16[20,8,5120]{2,1,0:T(8,128)(2,1)S(1)} %collective-permute-done.15) | copy-start | bytes 4915204
  89.8 52.7 %collective-permute-start.16 = (bf16[20,8,5120]{2,1,0:T(8,128)(2,1)S(1)}, bf16[20,8,5120]{2,1,0:T(8,128)(2,1)S(1)}, u32[]{:S(2)}, u32[]{:S(2)}) collective-permute-start(bf16[20,8,5120]{2,1,0:T(8,128)(2,1)S(1)} %collective-permute-done.15), channel_id=1, source_target_pairs={{0,4},{4,8},{8,12},{12,16},{16,20},{20,24},{24,28},{28,0},{1,5},{5... | collective-permute-start | bytes 4915208 | tf_op jit(solution)/shard_map/ppermute | solution.py:44
  107.4 52.7 %collective-permute-start.9 = (bf16[20,8,5120]{2,1,0:T(8,128)(2,1)S(1)}, bf16[20,8,5120]{2,1,0:T(8,128)(2,1)S(1)}, u32[]{:S(2)}, u32[]{:S(2)}) collective-permute-start(bf16[20,8,5120]{2,1,0:T(8,128)(2,1)S(1)} %collective-permute-done.8), channel_id=1, source_target_pairs={{0,4},{4,8},{8,12},{12,16},{16,20},{20,24},{24,28},{28,0},{1,5},{5... | collective-permute-start | bytes 4915208 | tf_op jit(solution)/shard_map/ppermute | solution.py:44
  126.1 51.5 %collective-permute-start.2 = (bf16[20,8,5120]{2,1,0:T(8,128)(2,1)S(1)}, bf16[20,8,5120]{2,1,0:T(8,128)(2,1)S(1)}, u32[]{:S(2)}, u32[]{:S(2)}) collective-permute-start(bf16[20,8,5120]{2,1,0:T(8,128)(2,1)S(1)} %collective-permute-done.1), channel_id=1, source_target_pairs={{0,4},{4,8},{8,12},{12,16},{16,20},{20,24},{24,28},{28,0},{1,5},{5... | collective-permute-start | bytes 4915208 | tf_op jit(solution)/shard_map/ppermute | solution.py:44
  142.5 105.4 %copy-start.12 = (bf16[20,8,5120]{2,1,0:T(8,128)(2,1)}, bf16[20,8,5120]{2,1,0:T(8,128)(2,1)S(1)}, u32[]{:S(2)}) copy-start(bf16[20,8,5120]{2,1,0:T(8,128)(2,1)S(1)} %collective-permute-done.16) | copy-start | bytes 4915204
  142.5 52.7 %collective-permute-start.17 = (bf16[20,8,5120]{2,1,0:T(8,128)(2,1)S(1)}, bf16[20,8,5120]{2,1,0:T(8,128)(2,1)S(1)}, u32[]{:S(2)}, u32[]{:S(2)}) collective-permute-start(bf16[20,8,5120]{2,1,0:T(8,128)(2,1)S(1)} %collective-permute-done.16), channel_id=1, source_target_pairs={{0,4},{4,8},{8,12},{12,16},{16,20},{20,24},{24,28},{28,0},{1,5},{5... | collective-permute-start | bytes 4915208 | tf_op jit(solution)/shard_map/ppermute | solution.py:44
  160.0 52.8 %collective-permute-start.10 = (bf16[20,8,5120]{2,1,0:T(8,128)(2,1)S(1)}, bf16[20,8,5120]{2,1,0:T(8,128)(2,1)}, u32[]{:S(2)}, u32[]{:S(2)}) collective-permute-start(bf16[20,8,5120]{2,1,0:T(8,128)(2,1)S(1)} %collective-permute-done.9), channel_id=1, source_target_pairs={{0,4},{4,8},{8,12},{12,16},{16,20},{20,24},{24,28},{28,0},{1,5},{5... | collective-permute-start | bytes 4915208 | tf_op jit(solution)/shard_map/ppermute | solution.py:44
  177.6 52.8 %collective-permute-start.3 = (bf16[20,8,5120]{2,1,0:T(8,128)(2,1)S(1)}, bf16[20,8,5120]{2,1,0:T(8,128)(2,1)}, u32[]{:S(2)}, u32[]{:S(2)}) collective-permute-start(bf16[20,8,5120]{2,1,0:T(8,128)(2,1)S(1)} %collective-permute-done.2), channel_id=1, source_target_pairs={{0,4},{4,8},{8,12},{12,16},{16,20},{20,24},{24,28},{28,0},{1,5},{5... | collective-permute-start | bytes 4915208 | tf_op jit(solution)/shard_map/ppermute | solution.py:44
  195.1 52.8 %collective-permute-start.18 = (bf16[20,8,5120]{2,1,0:T(8,128)(2,1)S(1)}, bf16[20,8,5120]{2,1,0:T(8,128)(2,1)}, u32[]{:S(2)}, u32[]{:S(2)}) collective-permute-start(bf16[20,8,5120]{2,1,0:T(8,128)(2,1)S(1)} %collective-permute-done.17), channel_id=1, source_target_pairs={{0,4},{4,8},{8,12},{12,16},{16,20},{20,24},{24,28},{28,0},{1,5},{5... | collective-permute-start | bytes 4915208 | tf_op jit(solution)/shard_map/ppermute | solution.py:44
  212.8 52.7 %collective-permute-start.11 = (bf16[20,8,5120]{2,1,0:T(8,128)(2,1)}, bf16[20,8,5120]{2,1,0:T(8,128)(2,1)}, u32[]{:S(2)}, u32[]{:S(2)}) collective-permute-start(bf16[20,8,5120]{2,1,0:T(8,128)(2,1)} %collective-permute-done.10), channel_id=1, source_target_pairs={{0,4},{4,8},{8,12},{12,16},{16,20},{20,24},{24,28},{28,0},{1,5},{5... | collective-permute-start | bytes 4915208 | tf_op jit(solution)/shard_map/ppermute | solution.py:44
  230.3 52.7 %collective-permute-start.4 = (bf16[20,8,5120]{2,1,0:T(8,128)(2,1)}, bf16[20,8,5120]{2,1,0:T(8,128)(2,1)}, u32[]{:S(2)}, u32[]{:S(2)}) collective-permute-start(bf16[20,8,5120]{2,1,0:T(8,128)(2,1)} %collective-permute-done.3), channel_id=1, source_target_pairs={{0,4},{4,8},{8,12},{12,16},{16,20},{20,24},{24,28},{28,0},{1,5},{5... | collective-permute-start | bytes 4915208 | tf_op jit(solution)/shard_map/ppermute | solution.py:44
  247.9 52.7 %collective-permute-start.19 = (bf16[20,8,5120]{2,1,0:T(8,128)(2,1)}, bf16[20,8,5120]{2,1,0:T(8,128)(2,1)}, u32[]{:S(2)}, u32[]{:S(2)}) collective-permute-start(bf16[20,8,5120]{2,1,0:T(8,128)(2,1)} %collective-permute-done.18), channel_id=1, source_target_pairs={{0,4},{4,8},{8,12},{12,16},{16,20},{20,24},{24,28},{28,0},{1,5},{5... | collective-permute-start | bytes 4915208 | tf_op jit(solution)/shard_map/ppermute | solution.py:44
  265.5 52.7 %collective-permute-start.12 = (bf16[20,8,5120]{2,1,0:T(8,128)(2,1)}, bf16[20,8,5120]{2,1,0:T(8,128)(2,1)}, u32[]{:S(2)}, u32[]{:S(2)}) collective-permute-start(bf16[20,8,5120]{2,1,0:T(8,128)(2,1)} %collective-permute-done.11), channel_id=1, source_target_pairs={{0,4},{4,8},{8,12},{12,16},{16,20},{20,24},{24,28},{28,0},{1,5},{5... | collective-permute-start | bytes 4915208 | tf_op jit(solution)/shard_map/ppermute | solution.py:44
  283.0 52.7 %collective-permute-start.5 = (bf16[20,8,5120]{2,1,0:T(8,128)(2,1)}, bf16[20,8,5120]{2,1,0:T(8,128)(2,1)}, u32[]{:S(2)}, u32[]{:S(2)}) collective-permute-start(bf16[20,8,5120]{2,1,0:T(8,128)(2,1)} %collective-permute-done.4), channel_id=1, source_target_pairs={{0,4},{4,8},{8,12},{12,16},{16,20},{20,24},{24,28},{28,0},{1,5},{5... | collective-permute-start | bytes 4915208 | tf_op jit(solution)/shard_map/ppermute | solution.py:44
  300.6 52.7 %collective-permute-start.20 = (bf16[20,8,5120]{2,1,0:T(8,128)(2,1)}, bf16[20,8,5120]{2,1,0:T(8,128)(2,1)}, u32[]{:S(2)}, u32[]{:S(2)}) collective-permute-start(bf16[20,8,5120]{2,1,0:T(8,128)(2,1)} %collective-permute-done.19), channel_id=1, source_target_pairs={{0,4},{4,8},{8,12},{12,16},{16,20},{20,24},{24,28},{28,0},{1,5},{5... | collective-permute-start | bytes 4915208 | tf_op jit(solution)/shard_map/ppermute | solution.py:44
  318.1 52.6 %collective-permute-start.13 = (bf16[20,8,5120]{2,1,0:T(8,128)(2,1)}, bf16[20,8,5120]{2,1,0:T(8,128)(2,1)S(1)}, u32[]{:S(2)}, u32[]{:S(2)}) collective-permute-start(bf16[20,8,5120]{2,1,0:T(8,128)(2,1)} %collective-permute-done.12), channel_id=1, source_target_pairs={{0,4},{4,8},{8,12},{12,16},{16,20},{20,24},{24,28},{28,0},{1,5},{5... | collective-permute-start | bytes 4915208 | tf_op jit(solution)/shard_map/ppermute | solution.py:44
  335.7 52.6 %collective-permute-start.6 = (bf16[20,8,5120]{2,1,0:T(8,128)(2,1)}, bf16[20,8,5120]{2,1,0:T(8,128)(2,1)S(1)}, u32[]{:S(2)}, u32[]{:S(2)}) collective-permute-start(bf16[20,8,5120]{2,1,0:T(8,128)(2,1)} %collective-permute-done.5), channel_id=1, source_target_pairs={{0,4},{4,8},{8,12},{12,16},{16,20},{20,24},{24,28},{28,0},{1,5},{5... | collective-permute-start | bytes 4915208 | tf_op jit(solution)/shard_map/ppermute | solution.py:44
  (17 other events, 565.6 us)
Sparse Core Ops, SparseCore 0:
  11.5 122.3 all-gather.6
  135.5 117.8 all-gather.8
  254.9 117.8 all-gather.10
